TPU v7x, 512 devices: a whole 4x4x16 slice. The times are simulated.
512 devices in a mesh: dom: 128 (over x, z, core), rep: 4 (over y).
Axes of the slice: x: 4, y: 4, z: 16, core: 2. Of those that a mesh axis runs over, the one named last changes fastest.
Arguments:
- features: float32 [128, 65536], P('rep', 'dom'), may hold values from -6 to 6
- tiles: bfloat16 [5120, 128, 128], P('dom'), may hold values from -0.25 to 0.25
- tile_row: int32 [5120], P('dom'), may hold values from 0 to 3
- tile_col: int32 [5120], P('dom'), may hold values from 0 to 511, as said below
- tile_count: int32 [128], P('dom'), may hold values from 16 to 40, as said below
- dest_slot: int32 [65536], P('dom'), may hold values from 0 to 65535, as said below
- w_in: bfloat16 [128, 1024], replicated, may hold values from -0.5 to 0.5
- w_mid: bfloat16 [1024, 1024], replicated, may hold values from -0.1875 to 0.1875
- w_out: bfloat16 [172, 1024], replicated, may hold values from -0.1875 to 0.1875
- cotangent: bfloat16 [172, 65536], P(None, ('dom', 'rep')), may hold values from -0.0234375 to 0.0234375
Outputs:
- batch_features: float32 [128, 65536], P(None, ('dom', 'rep'))
- grad_w_in: float32 [128, 1024], replicated
- grad_w_mid: float32 [1024, 1024], P('dom')
- grad_w_out: float32 [172, 1024], replicated
Inputs may be any that keep to these rules, and one draw needn't show every extreme that they name: `tile_col`: every slot of partition p, live or not, names a block column within 4 blocks of p's own blocks p * 4 to (p+1) * 4 - 1, counted modulo 512; each of the 8 blocks just before and just after p's own is named by one of p's first 8 slots. `tile_count`: counts vary from partition to partition (several partitions may share a count); at least one partition holds exactly 40 live slots. `dest_slot`: A permutation of the batch positions; each graph partition sends exactly 1 node into each block of 128 consecutive batch positions.
All inputs are finite; a program needn't handle non-finite values.
Results may differ from a plain program's by a relative error of at most 0.006.
Values sent between devices are 32-bit elements; how exact they have to be, the bound alone decides.
A program may use at most 64 MiB of HBM per device.

v0:
```python
import jax
import jax.numpy as jnp
from jax import lax
from jax.sharding import PartitionSpec as P

series_zero = 0.3085083
series_one = -0.4305395
series_two = 0.1864784
LEADING = (((0,), (0,)), ((), ()))
TRAILING = (((1,), (1,)), ((), ()))


def extended_2(cells, sides, width):
    for axis, dim in sides:
        count = lax.axis_size(axis)
        head = lax.slice_in_dim(cells, 0, width, axis=dim)
        tail = lax.slice_in_dim(cells, cells.shape[dim] - width, cells.shape[dim], axis=dim)
        cells = jnp.concatenate(
            [
                lax.ppermute(tail, axis, [(i, (i + 1) % count) for i in range(count)]),
                cells,
                lax.ppermute(head, axis, [((i + 1) % count, i) for i in range(count)]),
            ],
            axis=dim,
        )
    return cells


def silu_slope(pre):
    sigma = jax.nn.sigmoid(pre)
    return sigma * (1.0 + pre * (1.0 - sigma))


def neighbour_blocks(local, margin, tile_size):
    extended = extended_2(local, (("dom", 1),), margin * tile_size)
    return extended


def apply_operator(local, tiles_across, assignment_map, relative, margin):
    feature_count, node_count = local.shape
    tile_size = tiles_across.shape[1]
    extended = neighbour_blocks(local, margin, tile_size)
    blocks = extended.reshape(feature_count, -1, tile_size)
    input_values = jnp.take(blocks, relative, axis=1)
    block_products = jnp.einsum(
        "lkz,glz->glk", tiles_across, input_values, precision=lax.Precision.HIGHEST
    )
    final_result = jnp.einsum(
        "wy,kya->kwa", assignment_map, block_products, precision=lax.Precision.HIGHEST
    )
    return final_result.reshape(feature_count, node_count)


def shards(
    features, tiles, tile_row, tile_col, tile_count, dest_slot, w_in, w_mid, w_out, cotangent
):
    node_partition = lax.axis_index("dom")
    owners = lax.axis_size("dom")
    replicas = lax.axis_size("rep")
    feature_count, node_count = features.shape
    capacity = tiles.shape[0]
    tile_size = tiles.shape[1]
    block_count = node_count // tile_size
    total_blocks = block_count * owners
    relative = jnp.mod(tile_col - node_partition * block_count + block_count, total_blocks)
    live_mask = (jnp.arange(capacity, dtype=jnp.int32) < tile_count[0]).astype(jnp.float32)
    assignment_map = (
        tile_row[None, :] == jnp.arange(block_count, dtype=jnp.int32)[:, None]
    ).astype(jnp.float32) * live_mask[None, :]
    tiles_across = tiles.astype(jnp.float32)
    first = apply_operator(features, tiles_across, assignment_map, relative, block_count)
    second = (
        2.0 * apply_operator(first, tiles_across, assignment_map, relative, block_count) - features
    )
    diffused = series_zero * features + series_one * first + series_two * second
    segment = node_count // (owners * replicas)
    batch_rows = node_count // replicas
    sort_order = jnp.argsort(dest_slot)
    sorted_slots = jnp.take(dest_slot, sort_order)
    moved_rows = jnp.take(diffused, sort_order, axis=1).reshape(
        feature_count, owners, replicas, segment
    )
    moved_slots = sorted_slots.astype(jnp.float32).reshape(1, owners, replicas, segment)
    arrived, arrived_slots = (
        lax.all_to_all(
            lax.all_to_all(moved_rows, "dom", split_axis=1, concat_axis=1, tiled=True),
            "rep",
            split_axis=2,
            concat_axis=0,
            tiled=True,
        ),
        lax.all_to_all(
            lax.all_to_all(moved_slots, "dom", split_axis=1, concat_axis=1, tiled=True),
            "rep",
            split_axis=2,
            concat_axis=0,
            tiled=True,
        ),
    )
    owner_index = node_partition * replicas + lax.axis_index("rep")
    local_slots = arrived_slots[0].reshape(-1).astype(jnp.int32) - owner_index * batch_rows
    gathered = arrived.reshape(feature_count * replicas, -1)
    batch_features = jnp.zeros(gathered.shape, jnp.float32).at[:, local_slots].set(gathered)
    inputs_bf = batch_features.astype(jnp.bfloat16)
    pre_one = lax.dot_general(inputs_bf, w_in, LEADING, preferred_element_type=jnp.float32)
    hidden_one = jax.nn.silu(pre_one).astype(jnp.bfloat16)
    pre_two = jnp.dot(hidden_one, w_mid, preferred_element_type=jnp.float32)
    hidden_two = jax.nn.silu(pre_two).astype(jnp.bfloat16)
    grad_out = jnp.dot(cotangent, hidden_two, preferred_element_type=jnp.float32)
    back_two = lax.dot_general(cotangent, w_out, LEADING, preferred_element_type=jnp.float32)
    delta_two = (back_two * silu_slope(pre_two)).astype(jnp.bfloat16)
    back_one = lax.dot_general(delta_two, w_mid, TRAILING, preferred_element_type=jnp.float32)
    delta_one = (back_one * silu_slope(pre_one)).astype(jnp.bfloat16)
    grad_in = jnp.dot(inputs_bf, delta_one, preferred_element_type=jnp.float32)
    mid_shard = lax.psum_scatter(
        lax.dot_general(hidden_one, delta_two, LEADING, preferred_element_type=jnp.float32),
        "dom",
        scatter_dimension=0,
        tiled=True,
    )
    grad_mid = lax.psum(mid_shard, "rep")
    grad_in, grad_out = lax.psum((grad_in, grad_out), ("dom", "rep"))
    return (batch_features, grad_in, grad_mid, grad_out)


def solution(mesh):
    in_specs = (
        P("rep", "dom"),
        P("dom", None, None),
        P("dom"),
        P("dom"),
        P("dom"),
        P("dom"),
        P(),
        P(),
        P(),
        P(None, ("dom", "rep")),
    )
    out_specs = (P(None, ("dom", "rep")), P(), P("dom", None), P())
    return jax.shard_map(shards, mesh=mesh, in_specs=in_specs, out_specs=out_specs, check_vma=False)
```

profile of v0, /device:TPU:4, one launch (start us, length us, event | category | flops | bytes accessed | tf_op | source)
XLA Modules:
  0.0 604.7 jit_solution(3782618393977635226)
XLA Ops:
  8.0 0.0 copy-start
  8.0 0.0 copy-start.3
  8.0 2.2 collective-permute-start
  10.2 10.8 %collective-permute-start.1 = (f32[32,512]{1,0:T(8,128)}, f32[32,512]{1,0:T(8,128)}, u32[]{:S(2)}, u32[]{:S(2)}) collective-permute-start(f32[32,512]{1,0:T(8,128)} %param.12), channel_id=1, source_target_pairs={{4,0},{8,4},{12,8},{16,12},{20,16},{24,20},{28,24},{32,28},{36,32}... | collective-permute-start | bytes 196616 | tf_op jit(solution)/shard_map/ppermute | solution.py:22
  21.1 1.3 compare_and_fusion
  23.0 4.4 sort.17
  27.5 3.6 gather_fusion
  31.1 0.5 compare_convert_fusion
  31.6 1.5 copy_bitcast_fusion
  33.2 2.4 gather_fusion.2
  35.5 3.3 convolution_bitcast_fusion.2
  38.8 0.0 copy-done.6
  38.8 1.5 fusion.6
  40.3 0.6 copy.78
  40.9 1.9 collective-permute-start.2
  42.8 5.8 collective-permute-start.3
  48.6 0.7 convert_element_type.49
  49.4 13.3 %all-to-all-start = ((f32[1,128,4,1]{2,3,0,1:T(1,128)}), f32[1,128,4,1]{2,3,0,1:T(1,128)}, u32[]{:S(2)}, u32[]{:S(2)}) async-start(f32[1,128,4,1]{2,3,0,1:T(1,128)} %bitcast), calls=%async_computation | async-start | bytes 131072 | tf_op jit(solution)/shard_map/all_to_all | solution.py:93
  62.7 0.1 broadcast_in_dim.39
  62.8 0.9 concatenate.12
  63.7 1.5 concatenate.13
  65.2 0.9 pad_maximum_fusion
  66.1 0.7 copy.59
  66.8 2.5 gather_fusion.3
  69.3 3.3 convolution_bitcast_fusion.1
  72.6 0.0 copy-done.7
  72.6 0.0 copy-start.2
  72.6 0.8 convolution_multiply_fusion.2
  73.5 0.1 copy.61
  73.6 1.2 gather_fusion.1
  74.8 0.2 fusion.47
  75.0 0.8 reshape.166
  75.9 0.6 all-to-all-done
  76.4 15.6 %all-to-all-start.2 = ((f32[128,1,128]{2,1,0:T(1,128)}), f32[128,1,128]{2,1,0:T(1,128)S(1)}, u32[]{:S(2)}, u32[]{:S(2)}) async-start(f32[128,1,128]{2,1,0:T(1,128)} %reshape.166), calls=%async_computation.2 | async-start | bytes 131072 | tf_op jit(solution)/shard_map/all_to_all | solution.py:86
  92.1 1.5 copy.56
  93.5 12.6 %all-to-all-done.2 = f32[128,1,128]{2,1,0:T(1,128)S(1)} async-done(((f32[128,1,128]{2,1,0:T(1,128)}), f32[128,1,128]{2,1,0:T(1,128)S(1)}, u32[]{:S(2)}, u32[]{:S(2)}) %all-to-all-start.2) | async-done | bytes 65568 | tf_op jit(solution)/shard_map/all_to_all | solution.py:86
  106.2 4.5 all-to-all-start.1
  110.6 0.5 broadcast.141
  111.1 0.8 reduce
  111.9 0.2 reshape.167
  112.1 0.7 copy.63
  112.9 2.9 all-to-all-done.1
  115.8 3.3 all-to-all-start.3
  119.1 0.0 reduce-scatter.2.cloned.1.call-start
  119.2 5.5 all-to-all-done.3
  124.7 0.1 copy.64
  124.8 0.9 scatter_custom_fusion
  125.7 0.2 fusion.25
  125.9 0.0 copy-start.10
  125.9 0.5 fusion.46
  126.4 0.5 copy-done.10
  126.9 0.3 fusion
  127.2 2.7 fusion.45
  129.9 0.0 reduce-scatter.2.cloned.1.call-update
  130.0 0.0 all-reduce.3.cloned.1.call-start
  130.0 1.2 convolution_bitcast_fusion
  131.2 1.8 fusion.2
  133.0 0.0 all-reduce.3.cloned.1.call-update
  133.1 0.7 copy.65
  133.8 249.1 %reduce-scatter.2.cloned.1.call-done = f32[8,1024]{1,0:T(8,128)} async-done(((f32[1024,1024]{1,0:T(8,128)}), f32[8,1024]{1,0:T(8,128)}) %reduce-scatter.2.cloned.1.call-update) | async-done | bytes 32784 | tf_op jit(solution)/shard_map/reduce_scatter | solution.py:115
  382.9 18.2 %psum.22 = f32[8,1024]{1,0:T(8,128)} all-reduce(f32[8,1024]{1,0:T(8,128)} %reduce-scatter.2.cloned.1.call-done), channel_id=1, replica_groups=mesh['dom'=128,'rep'=4] {'rep'}, use_global_device_ids=true, to_apply=%region_4.6 | all-reduce | flops 8192 | bytes 65536 | tf_op jit(solution)/shard_map/psum | solution.py:121
  401.1 192.3 %all-reduce.3.cloned.1.call-done = (f32[128,1024]{1,0:T(8,128)}, f32[172,1024]{1,0:T(8,128)}) async-done(((f32[128,1024]{1,0:T(8,128)}, f32[172,1024]{1,0:T(8,128)}), (f32[128,1024]{1,0:T(8,128)}, f32[172,1024]{1,0:T(8,128)})) %all-reduce.3.cloned.1.call-update) | async-done | bytes 1228816 | tf_op jit(solution)/shard_map/psum | solution.py:122
  593.3 1.9 copy.82
  595.2 2.0 copy.83
  (28 shorter events, 0.1 us)
Async XLA Ops:
  8.0 117.9 %copy-start = (bf16[1024,1024]{1,0:T(8,128)(2,1)S(1)}, bf16[1024,1024]{1,0:T(8,128)(2,1)}, u32[]{:S(2)}) copy-start(bf16[1024,1024]{1,0:T(8,128)(2,1)} %param.19) | copy-start | bytes 6291460
  8.0 23.6 %copy-start.3 = (f32[32,512]{1,0:T(8,128)S(1)}, f32[32,512]{1,0:T(8,128)}, u32[]{:S(2)}) copy-start(f32[32,512]{1,0:T(8,128)} %param.12) | copy-start | bytes 196612
  8.0 27.5 %copy-start.1 = (bf16[40,128,128]{2,1,0:T(8,128)(2,1)S(1)}, bf16[40,128,128]{2,1,0:T(8,128)(2,1)}, u32[]{:S(2)}) copy-start(bf16[40,128,128]{2,1,0:T(8,128)(2,1)} %param.13) | copy-start | bytes 3932164
  8.0 23.6 %collective-permute-start = (f32[32,512]{1,0:T(8,128)}, f32[32,512]{1,0:T(8,128)S(1)}, u32[]{:S(2)}, u32[]{:S(2)}) collective-permute-start(f32[32,512]{1,0:T(8,128)} %param.12), channel_id=1, source_target_pairs={{0,4},{4,8},{8,12},{12,16},{16,20},{20,24},{24,28},{28,32},{32,36}... | collective-permute-start | bytes 196616 | tf_op jit(solution)/shard_map/ppermute | solution.py:20
  10.2 21.4 %collective-permute-start.1 = (f32[32,512]{1,0:T(8,128)}, f32[32,512]{1,0:T(8,128)}, u32[]{:S(2)}, u32[]{:S(2)}) collective-permute-start(f32[32,512]{1,0:T(8,128)} %param.12), channel_id=1, source_target_pairs={{4,0},{8,4},{12,8},{16,12},{20,16},{24,20},{28,24},{32,28},{36,32}... | collective-permute-start | bytes 196616 | tf_op jit(solution)/shard_map/ppermute | solution.py:22
  22.3 16.5 %copy-start.6 = (s32[1024]{0:T(1024)}, s32[1024]{0:T(1024)S(1)}, u32[]{:S(2)}) copy-start(s32[1024]{0:T(1024)S(1)} %pad_clamp_fusion) | copy-start | bytes 12292
  27.5 11.3 %copy-start.5 = (s32[1024]{0:T(1024)}, s32[1024]{0:T(1024)S(1)}, u32[]{:S(2)}) copy-start(s32[1024]{0:T(1024)S(1)} %pad_clamp_fusion.1) | copy-start | bytes 12292
  33.2 5.7 copy-start.8
  40.9 21.9 %collective-permute-start.2 = (f32[32,512]{1,0:T(8,128)}, f32[32,512]{1,0:T(8,128)}, u32[]{:S(2)}, u32[]{:S(2)}) collective-permute-start(f32[32,512]{1,0:T(8,128)} %bitcast.70), channel_id=1, source_target_pairs={{0,4},{4,8},{8,12},{12,16},{16,20},{20,24},{24,28},{28,32},{32,36}... | collective-permute-start | bytes 196616 | tf_op jit(solution)/shard_map/ppermute | solution.py:20
  42.8 20.8 %collective-permute-start.3 = (f32[32,512]{1,0:T(8,128)}, f32[32,512]{1,0:T(8,128)}, u32[]{:S(2)}, u32[]{:S(2)}) collective-permute-start(f32[32,512]{1,0:T(8,128)} %bitcast.70), channel_id=1, source_target_pairs={{4,0},{8,4},{12,8},{16,12},{20,16},{24,20},{28,24},{32,28},{36,32}... | collective-permute-start | bytes 196616 | tf_op jit(solution)/shard_map/ppermute | solution.py:22
  49.4 27.1 %all-to-all-start = ((f32[1,128,4,1]{2,3,0,1:T(1,128)}), f32[1,128,4,1]{2,3,0,1:T(1,128)}, u32[]{:S(2)}, u32[]{:S(2)}) async-start(f32[1,128,4,1]{2,3,0,1:T(1,128)} %bitcast), calls=%async_computation | async-start | bytes 131072 | tf_op jit(solution)/shard_map/all_to_all | solution.py:93
  66.8 6.7 %copy-start.4 = (f32[32,512]{1,0:T(8,128)S(1)}, f32[32,512]{1,0:T(8,128)}, u32[]{:S(2)}) copy-start(f32[32,512]{1,0:T(8,128)} %param.12) | copy-start | bytes 196612
  69.3 3.3 copy-start.7
  69.3 3.3 copy-start.9
  72.6 53.1 %copy-start.2 = (bf16[128,1024]{1,0:T(8,128)(2,1)S(1)}, bf16[128,1024]{1,0:T(8,128)(2,1)}, u32[]{:S(2)}) copy-start(bf16[128,1024]{1,0:T(8,128)(2,1)} %param.18) | copy-start | bytes 786436
  76.4 29.7 %all-to-all-start.2 = ((f32[128,1,128]{2,1,0:T(1,128)}), f32[128,1,128]{2,1,0:T(1,128)S(1)}, u32[]{:S(2)}, u32[]{:S(2)}) async-start(f32[128,1,128]{2,1,0:T(1,128)} %reshape.166), calls=%async_computation.2 | async-start | bytes 131072 | tf_op jit(solution)/shard_map/all_to_all | solution.py:86
  106.2 9.6 %all-to-all-start.1 = ((f32[1,128,4,1]{1,3,0,2:T(1,128)}), f32[1,128,4,1]{1,3,0,2:T(1,128)S(1)}, u32[]{:S(2)}, u32[]{:S(2)}) async-start(f32[1,128,4,1]{1,3,0,2:T(1,128)} %copy.56), calls=%async_computation.1 | async-start | bytes 4096 | tf_op jit(solution)/shard_map/all_to_all | solution.py:92
  115.8 8.9 %all-to-all-start.3 = ((f32[32,128,4,1]{1,0,3,2:T(8,128)}), f32[32,128,4,1]{1,0,3,2:T(8,128)S(1)}, u32[]{:S(2)}, u32[]{:S(2)}) async-start(f32[32,128,4,1]{1,0,3,2:T(8,128)} %copy.63), calls=%async_computation.3 | async-start | bytes 131072 | tf_op jit(solution)/shard_map/all_to_all | solution.py:85
  119.1 263.8 %reduce-scatter.2.cloned.1.call-start = ((), (), s32[]{:S(2)}) async-start(), calls=%async_computation.5 | async-start | bytes 4227072 | tf_op jit(solution)/shard_map/reduce_scatter | solution.py:115
  125.9 1.0 copy-start.10
  125.9 1.0 copy-start.11
  130.0 463.4 %all-reduce.3.cloned.1.call-start = ((), (), s32[]{:S(2)}) async-start(), calls=%async_computation.6 | async-start | bytes 2490368 | tf_op jit(solution)/shard_map/psum | solution.py:122
Sparse Core Ops, SparseCore 0:
  130.1 252.7 reduce-scatter.1
Sparse Core Ops, SparseCore 1:
  136.5 456.8 all-reduce.2
where the time goes:
time: 606 us; the launch traced here: 605 us
  waiting for transfers between devices  463 us (76%)
  starting transfers between devices  57.4 us (9%)
  local copies, waits for them, and re-layouts  24.3 us (4%)
  blocking collectives  18.2 us (3%)
  between operations  16.5 us (3%)
  matrix products  15.5 us (3%)
  other arithmetic  9.71 us (2%)
    reduce_scatter x1, waiting for transfers between devices, shards(): lax.psum_scatter(lax.dot_general(hidden_one, delta_two, LEADING, preferre...  249 us
    psum x1, waiting for transfers between devices, shards(): grad_in, grad_out = lax.psum((grad_in, grad_out), ('dom', 'rep'))  192 us
    psum x1, blocking collectives, shards(): grad_mid = lax.psum(mid_shard, 'rep')  18.2 us
    ppermute x2, starting transfers between devices, extended_2(): lax.ppermute(head, axis, [((i + 1) % count, i) for i in range(count)])  16.6 us
    all_to_all x1, starting transfers between devices, shards(): lax.all_to_all(moved_rows, 'dom', split_axis=1, concat_axis=1, tiled=True)  15.6 us
    all_to_all x1, starting transfers between devices, shards(): lax.all_to_all(moved_slots, 'dom', split_axis=1, concat_axis=1, tiled=True)  13.3 us
    all_to_all x1, waiting for transfers between devices, shards(): lax.all_to_all(moved_rows, 'dom', split_axis=1, concat_axis=1, tiled=True)  12.6 us
  transfers between devices with their start and end apart: 10, of which 6 were waited for; matrix products, arithmetic and copies ran while one was open for 5% of the time, Pallas kernels for 0%

commit v1 on v0

--- a/solution.py
+++ b/solution.py
@@ -118,7 +118,9 @@
         scatter_dimension=0,
         tiled=True,
     )
-    grad_mid = lax.psum(mid_shard, "rep")
+    grad_mid = mid_shard
+    for hop in (1, 2):
+        grad_mid = grad_mid + lax.ppermute(grad_mid, "rep", [(dev, dev ^ hop) for dev in range(4)])
     grad_in, grad_out = lax.psum((grad_in, grad_out), ("dom", "rep"))
     return (batch_features, grad_in, grad_mid, grad_out)
 

time: 606 us -> 606 us (level)
  blocking collectives: 18.2 us -> 0 us
  starting transfers between devices: 57.4 us -> 65.9 us
  waiting for transfers between devices: 463 us -> 471 us
    psum x1 -> x0, blocking collectives: 18.2 us -> none  [shards(): grad_mid = lax.psum(mid_shard, 'rep')]
    ppermute x0 -> x2, starting transfers between devices: none -> 8.31 us  [shards(): lax.ppermute(grad_mid, 'rep', [(dev, dev ^ hop) for dev in range(4)])]
  transfers between devices with their start and end apart: 10 -> 12, of which waited for: 6 -> 8; matrix products, arithmetic and copies ran while one was open for 5% -> 5% of each run, Pallas kernels for 0% -> 0%
where the time goes in v1:
time: 606 us; the launch traced here: 605 us
  waiting for transfers between devices  471 us (78%)
  starting transfers between devices  65.9 us (11%)
  local copies, waits for them, and re-layouts  24.3 us (4%)
  between operations  16.5 us (3%)
  matrix products  15.5 us (3%)
  other arithmetic  11.1 us (2%)
    reduce_scatter x1, waiting for transfers between devices, shards(): lax.psum_scatter(lax.dot_general(hidden_one, delta_two, LEADING, preferre...  250 us
    psum x1, waiting for transfers between devices, shards(): grad_in, grad_out = lax.psum((grad_in, grad_out), ('dom', 'rep'))  196 us
    ppermute x2, starting transfers between devices, extended_2(): lax.ppermute(head, axis, [((i + 1) % count, i) for i in range(count)])  16.6 us
    all_to_all x1, starting transfers between devices, shards(): lax.all_to_all(moved_rows, 'dom', split_axis=1, concat_axis=1, tiled=True)  15.8 us
    all_to_all x1, starting transfers between devices, shards(): lax.all_to_all(moved_slots, 'dom', split_axis=1, concat_axis=1, tiled=True)  13.3 us
    all_to_all x1, waiting for transfers between devices, shards(): lax.all_to_all(moved_rows, 'dom', split_axis=1, concat_axis=1, tiled=True)  12.6 us
  transfers between devices with their start and end apart: 12, of which 8 were waited for; matrix products, arithmetic and copies ran while one was open for 5% of the time, Pallas kernels for 0%

profile of v1, /device:TPU:4, one launch (start us, length us, event | category | flops | bytes accessed | tf_op | source)
XLA Modules:
  0.0 604.9 jit_solution(6974166318082358645)
XLA Ops:
  8.0 2.2 collective-permute-start
  10.2 10.8 %collective-permute-start.1 = (f32[32,512]{1,0:T(8,128)}, f32[32,512]{1,0:T(8,128)}, u32[]{:S(2)}, u32[]{:S(2)}) collective-permute-start(f32[32,512]{1,0:T(8,128)} %param.12), channel_id=1, source_target_pairs={{4,0},{8,4},{12,8},{16,12},{20,16},{24,20},{28,24},{32,28},{36,32}... | collective-permute-start | bytes 196616 | tf_op jit(solution)/shard_map/ppermute | solution.py:22
  21.1 1.2 compare_and_fusion
  22.9 4.4 sort.17
  27.4 3.6 gather_fusion
  31.0 0.6 compare_convert_fusion
  31.6 1.5 copy_bitcast_fusion
  33.2 2.4 gather_fusion.2
  35.5 3.3 convolution_bitcast_fusion.2
  38.8 0.0 copy-done.6
  38.8 1.5 fusion.6
  40.3 0.6 copy.78
  41.0 1.9 collective-permute-start.2
  42.9 5.8 collective-permute-start.3
  48.6 0.7 convert_element_type.49
  49.4 13.3 %all-to-all-start = ((f32[1,128,4,1]{2,3,0,1:T(1,128)}), f32[1,128,4,1]{2,3,0,1:T(1,128)}, u32[]{:S(2)}, u32[]{:S(2)}) async-start(f32[1,128,4,1]{2,3,0,1:T(1,128)} %bitcast), calls=%async_computation | async-start | bytes 131072 | tf_op jit(solution)/shard_map/all_to_all | solution.py:93
  62.7 0.1 broadcast_in_dim.39
  62.8 0.9 concatenate.12
  63.7 1.5 concatenate.13
  65.2 0.9 pad_maximum_fusion
  66.1 0.7 copy.59
  66.8 2.5 gather_fusion.3
  69.3 3.3 convolution_bitcast_fusion.1
  72.7 0.8 convolution_multiply_fusion.2
  73.5 0.1 copy.61
  73.7 1.2 gather_fusion.1
  74.8 0.2 fusion.47
  75.1 0.8 reshape.166
  75.9 0.4 all-to-all-done
  76.3 15.8 %all-to-all-start.2 = ((f32[128,1,128]{2,1,0:T(1,128)}), f32[128,1,128]{2,1,0:T(1,128)S(1)}, u32[]{:S(2)}, u32[]{:S(2)}) async-start(f32[128,1,128]{2,1,0:T(1,128)} %reshape.166), calls=%async_computation.2 | async-start | bytes 131072 | tf_op jit(solution)/shard_map/all_to_all | solution.py:86
  92.1 1.5 copy.56
  93.6 12.6 %all-to-all-done.2 = f32[128,1,128]{2,1,0:T(1,128)S(1)} async-done(((f32[128,1,128]{2,1,0:T(1,128)}), f32[128,1,128]{2,1,0:T(1,128)S(1)}, u32[]{:S(2)}, u32[]{:S(2)}) %all-to-all-start.2) | async-done | bytes 65568 | tf_op jit(solution)/shard_map/all_to_all | solution.py:86
  106.2 4.5 all-to-all-start.1
  110.6 0.5 broadcast.141
  111.2 0.8 reduce
  112.0 0.2 reshape.167
  112.1 0.7 copy.63
  112.9 2.9 all-to-all-done.1
  115.8 3.3 all-to-all-start.3
  119.1 0.0 reduce-scatter.2.cloned.1.call-start
  119.2 5.5 all-to-all-done.3
  124.7 0.1 copy.64
  124.8 0.9 scatter_custom_fusion
  125.7 0.2 fusion.25
  126.0 0.4 fusion.46
  126.4 0.5 copy-done.10
  126.9 0.3 fusion
  127.3 2.7 fusion.45
  130.0 0.0 reduce-scatter.2.cloned.1.call-update
  130.0 0.0 all-reduce.3.cloned.1.call-start
  130.1 1.2 convolution_bitcast_fusion
  131.3 1.8 fusion.2
  133.1 0.0 all-reduce.3.cloned.1.call-update
  133.1 249.9 %reduce-scatter.2.cloned.1.call-done = f32[8,1024]{1,0:T(8,128)} async-done(((f32[1024,1024]{1,0:T(8,128)}), f32[8,1024]{1,0:T(8,128)}) %reduce-scatter.2.cloned.1.call-update) | async-done | bytes 32784 | tf_op jit(solution)/shard_map/reduce_scatter | solution.py:115
  383.0 3.4 collective-permute-start.4
  386.4 2.6 collective-permute-done.4
  389.0 0.8 add.93
  389.8 4.9 collective-permute-start.5
  394.7 0.7 copy.65
  395.4 1.6 collective-permute-done.5
  397.1 0.6 add.94
  397.7 195.8 %all-reduce.3.cloned.1.call-done = (f32[128,1024]{1,0:T(8,128)}, f32[172,1024]{1,0:T(8,128)}) async-done(((f32[128,1024]{1,0:T(8,128)}, f32[172,1024]{1,0:T(8,128)}), (f32[128,1024]{1,0:T(8,128)}, f32[172,1024]{1,0:T(8,128)})) %all-reduce.3.cloned.1.call-update) | async-done | bytes 1228816 | tf_op jit(solution)/shard_map/psum | solution.py:124
  593.5 1.9 copy.82
  595.4 2.0 copy.83
  (33 shorter events, 0.1 us)
Async XLA Ops:
  8.0 117.9 %copy-start = (bf16[1024,1024]{1,0:T(8,128)(2,1)S(1)}, bf16[1024,1024]{1,0:T(8,128)(2,1)}, u32[]{:S(2)}) copy-start(bf16[1024,1024]{1,0:T(8,128)(2,1)} %param.19) | copy-start | bytes 6291460
  8.0 23.6 %copy-start.3 = (f32[32,512]{1,0:T(8,128)S(1)}, f32[32,512]{1,0:T(8,128)}, u32[]{:S(2)}) copy-start(f32[32,512]{1,0:T(8,128)} %param.12) | copy-start | bytes 196612
  8.0 27.5 %copy-start.1 = (bf16[40,128,128]{2,1,0:T(8,128)(2,1)S(1)}, bf16[40,128,128]{2,1,0:T(8,128)(2,1)}, u32[]{:S(2)}) copy-start(bf16[40,128,128]{2,1,0:T(8,128)(2,1)} %param.13) | copy-start | bytes 3932164
  8.0 23.6 %collective-permute-start = (f32[32,512]{1,0:T(8,128)}, f32[32,512]{1,0:T(8,128)S(1)}, u32[]{:S(2)}, u32[]{:S(2)}) collective-permute-start(f32[32,512]{1,0:T(8,128)} %param.12), channel_id=1, source_target_pairs={{0,4},{4,8},{8,12},{12,16},{16,20},{20,24},{24,28},{28,32},{32,36}... | collective-permute-start | bytes 196616 | tf_op jit(solution)/shard_map/ppermute | solution.py:20
  10.2 21.4 %collective-permute-start.1 = (f32[32,512]{1,0:T(8,128)}, f32[32,512]{1,0:T(8,128)}, u32[]{:S(2)}, u32[]{:S(2)}) collective-permute-start(f32[32,512]{1,0:T(8,128)} %param.12), channel_id=1, source_target_pairs={{4,0},{8,4},{12,8},{16,12},{20,16},{24,20},{28,24},{32,28},{36,32}... | collective-permute-start | bytes 196616 | tf_op jit(solution)/shard_map/ppermute | solution.py:22
  22.3 16.5 %copy-start.6 = (s32[1024]{0:T(1024)}, s32[1024]{0:T(1024)S(1)}, u32[]{:S(2)}) copy-start(s32[1024]{0:T(1024)S(1)} %pad_clamp_fusion) | copy-start | bytes 12292
  27.4 11.4 %copy-start.5 = (s32[1024]{0:T(1024)}, s32[1024]{0:T(1024)S(1)}, u32[]{:S(2)}) copy-start(s32[1024]{0:T(1024)S(1)} %pad_clamp_fusion.1) | copy-start | bytes 12292
  33.2 5.7 copy-start.8
  41.0 21.9 %collective-permute-start.2 = (f32[32,512]{1,0:T(8,128)}, f32[32,512]{1,0:T(8,128)}, u32[]{:S(2)}, u32[]{:S(2)}) collective-permute-start(f32[32,512]{1,0:T(8,128)} %bitcast.70), channel_id=1, source_target_pairs={{0,4},{4,8},{8,12},{12,16},{16,20},{20,24},{24,28},{28,32},{32,36}... | collective-permute-start | bytes 196616 | tf_op jit(solution)/shard_map/ppermute | solution.py:20
  42.9 20.8 %collective-permute-start.3 = (f32[32,512]{1,0:T(8,128)}, f32[32,512]{1,0:T(8,128)}, u32[]{:S(2)}, u32[]{:S(2)}) collective-permute-start(f32[32,512]{1,0:T(8,128)} %bitcast.70), channel_id=1, source_target_pairs={{4,0},{8,4},{12,8},{16,12},{20,16},{24,20},{28,24},{32,28},{36,32}... | collective-permute-start | bytes 196616 | tf_op jit(solution)/shard_map/ppermute | solution.py:22
  49.4 26.9 %all-to-all-start = ((f32[1,128,4,1]{2,3,0,1:T(1,128)}), f32[1,128,4,1]{2,3,0,1:T(1,128)}, u32[]{:S(2)}, u32[]{:S(2)}) async-start(f32[1,128,4,1]{2,3,0,1:T(1,128)} %bitcast), calls=%async_computation | async-start | bytes 131072 | tf_op jit(solution)/shard_map/all_to_all | solution.py:93
  66.8 6.7 %copy-start.4 = (f32[32,512]{1,0:T(8,128)S(1)}, f32[32,512]{1,0:T(8,128)}, u32[]{:S(2)}) copy-start(f32[32,512]{1,0:T(8,128)} %param.12) | copy-start | bytes 196612
  69.3 3.3 copy-start.7
  69.3 3.3 copy-start.9
  72.7 53.1 %copy-start.2 = (bf16[128,1024]{1,0:T(8,128)(2,1)S(1)}, bf16[128,1024]{1,0:T(8,128)(2,1)}, u32[]{:S(2)}) copy-start(bf16[128,1024]{1,0:T(8,128)(2,1)} %param.18) | copy-start | bytes 786436
  76.3 29.9 %all-to-all-start.2 = ((f32[128,1,128]{2,1,0:T(1,128)}), f32[128,1,128]{2,1,0:T(1,128)S(1)}, u32[]{:S(2)}, u32[]{:S(2)}) async-start(f32[128,1,128]{2,1,0:T(1,128)} %reshape.166), calls=%async_computation.2 | async-start | bytes 131072 | tf_op jit(solution)/shard_map/all_to_all | solution.py:86
  106.2 9.6 %all-to-all-start.1 = ((f32[1,128,4,1]{1,3,0,2:T(1,128)}), f32[1,128,4,1]{1,3,0,2:T(1,128)S(1)}, u32[]{:S(2)}, u32[]{:S(2)}) async-start(f32[1,128,4,1]{1,3,0,2:T(1,128)} %copy.56), calls=%async_computation.1 | async-start | bytes 4096 | tf_op jit(solution)/shard_map/all_to_all | solution.py:92
  115.8 8.9 %all-to-all-start.3 = ((f32[32,128,4,1]{1,0,3,2:T(8,128)}), f32[32,128,4,1]{1,0,3,2:T(8,128)S(1)}, u32[]{:S(2)}, u32[]{:S(2)}) async-start(f32[32,128,4,1]{1,0,3,2:T(8,128)} %copy.63), calls=%async_computation.3 | async-start | bytes 131072 | tf_op jit(solution)/shard_map/all_to_all | solution.py:85
  119.1 263.9 %reduce-scatter.2.cloned.1.call-start = ((), (), s32[]{:S(2)}) async-start(), calls=%async_computation.5 | async-start | bytes 4227072 | tf_op jit(solution)/shard_map/reduce_scatter | solution.py:115
  126.0 1.0 copy-start.10
  126.0 1.0 copy-start.11
  130.0 463.5 %all-reduce.3.cloned.1.call-start = ((), (), s32[]{:S(2)}) async-start(), calls=%async_computation.6 | async-start | bytes 2490368 | tf_op jit(solution)/shard_map/psum | solution.py:124
  383.0 6.0 collective-permute-start.4
  389.8 7.3 %collective-permute-start.5 = (f32[8,1024]{1,0:T(8,128)S(1)}, f32[8,1024]{1,0:T(8,128)S(1)}, u32[]{:S(2)}, u32[]{:S(2)}) collective-permute-start(f32[8,1024]{1,0:T(8,128)S(1)} %add.93), channel_id=1, source_target_pairs={{0,2},{1,3},{2,0},{3,1},{4,6},{5,7},{6,4},{7,5},{8,10},{9,11},{10,... | collective-permute-start | bytes 98312 | tf_op jit(solution)/shard_map/ppermute | solution.py:123
Sparse Core Ops, SparseCore 0:
  130.1 252.8 reduce-scatter.1
Sparse Core Ops, SparseCore 1:
  136.6 456.9 all-reduce.2
